TPU v7x, 512 devices: a whole 4x4x16 slice. The times are simulated.
512 devices in a mesh: pair: 64 (over x, z), virt: 8 (over y, core).
Axes of the slice: x: 4, y: 4, z: 16, core: 2. Of those that a mesh axis runs over, the one named last changes fastest.
Arguments:
- t2_amplitudes: float32 [256, 8192], P('pair', 'virt'), may hold values from -6 to 6
- integral_tiles: float32 [64, 8, 32, 128, 128], P('pair', 'virt'), may hold values from -0.0625 to 0.0625
- out_tiles: int32 [64, 8, 32], P('pair', 'virt'), may hold values from 0 to 63, as said below
- in_tiles: int32 [64, 8, 32], P('pair', 'virt'), may hold values from 0 to 63
- tile_counts: int32 [64, 8], P('pair', 'virt'), may hold values from 1 to 32, as said below
Outputs:
- ladder: float32 [256, 8192], P('pair', 'virt')
Inputs may be any that keep to these rules, and one draw needn't show every extreme that they name: `out_tiles`: slots of the devices at virt index v name output tiles v * 8 to (v + 1) * 8 - 1 only. `tile_counts`: in every draw some device has all 32 slots live.
All inputs are finite; a program needn't handle non-finite values.
Results may differ from a plain program's by a relative error of at most 0.0003.
Values sent between devices are 32-bit elements; how exact they have to be, the bound alone decides.
A program may use at most 64 MiB of HBM per device.

v0:
```python
import jax
import jax.numpy as jnp
from jax import lax
from jax.sharding import PartitionSpec as P

W = 128


def shards(t2_amplitudes, integral_tiles, out_tiles, in_tiles, tile_counts):
    rows_dev = t2_amplitudes.shape[0]
    slab_cols = t2_amplitudes.shape[1]
    local_tiles = slab_cols // W
    gathered_rows = lax.all_gather(t2_amplitudes, "pair", axis=0, tiled=True)
    whole = lax.all_gather(gathered_rows, "virt", axis=1, tiled=True)
    total_rows = whole.shape[0]
    group_tiles = whole.shape[1] // W
    blocks = whole.reshape(total_rows, group_tiles, W)
    slot_total = integral_tiles.shape[2]
    tiles = integral_tiles.reshape(slot_total, W, W)
    flat_outs = out_tiles.reshape(slot_total)
    flat_ins = in_tiles.reshape(slot_total)
    count = tile_counts.reshape(-1)[0]
    virt_index = lax.axis_index("virt")
    slot_group = 8
    group_steps = (count + slot_group - 1) // slot_group

    def one_group(index, totals):
        offset = index * slot_group
        ins = lax.dynamic_slice_in_dim(flat_ins, offset, slot_group)
        outs = lax.dynamic_slice_in_dim(flat_outs, offset, slot_group)
        group_tiles_now = lax.dynamic_slice_in_dim(tiles, offset, slot_group, 0)
        columns = jnp.take(blocks, ins, axis=1)
        product = jnp.einsum(
            "psc,sca->psa", columns, group_tiles_now, precision=lax.Precision.HIGHEST
        )
        is_live = offset + jnp.arange(slot_group, dtype=jnp.int32) < count
        local_ids = outs - virt_index * local_tiles
        selector = (
            (local_ids[:, None] == jnp.arange(local_tiles, dtype=jnp.int32)[None, :])
            & is_live[:, None]
        ).astype(jnp.float32)
        return totals + jnp.einsum(
            "psa,sk->pka", product, selector, precision=lax.Precision.HIGHEST
        )

    start_totals = jnp.zeros((total_rows, local_tiles, W), jnp.float32)
    totals = lax.fori_loop(0, group_steps, one_group, start_totals)
    partial_sums = totals.reshape(total_rows, slab_cols)
    summed = lax.psum(partial_sums, "pair")
    first_row = lax.axis_index("pair") * rows_dev
    return lax.dynamic_slice_in_dim(summed, first_row, rows_dev, 0)


def solution(mesh):
    return jax.shard_map(
        shards,
        mesh=mesh,
        in_specs=(
            P("pair", "virt"),
            P("pair", "virt", None, None, None),
            P("pair", "virt", None),
            P("pair", "virt", None),
            P("pair", "virt"),
        ),
        out_specs=P("pair", "virt"),
        check_vma=False,
    )
```

profile of v0, /device:TPU:1, one launch (start us, length us, event | category | flops | bytes accessed | tf_op | source)
XLA Modules:
  0.0 535.0 jit_solution(1411696251952802740)
XLA Ops:
  6.5 0.7 all-gather.6.cloned.1.call-update
  7.3 137.8 %all-gather.6.cloned.1.call-done = f32[64,4,1024]{2,1,0:T(4,128)} async-done(((f32[1,4,1024]{2,1,0:T(4,128)}), f32[64,4,1024]{2,1,0:T(4,128)}) %all-gather.6.cloned.1.call-update) | async-done | bytes 1048592 | tf_op jit(solution)/shard_map/all_gather | solution.py:13
  145.1 2.7 reshape.41
  148.5 2.9 copy.15
  151.4 59.9 %all-gather.4.cloned.1.call-done = f32[256,8192]{1,0:T(8,128)} async-done(((f32[256,1024]{1,0:T(8,128)}), f32[256,8192]{1,0:T(8,128)}) %all-gather.4.cloned.1.call-update) | async-done | bytes 8388624 | tf_op jit(solution)/shard_map/all_gather | solution.py:14
  211.3 9.0 %copy.16 = f32[256,8192]{0,1:T(8,128)} copy(f32[256,8192]{1,0:T(8,128)} %all-gather.4.cloned.1.call-done) | data formatting | bytes 16777216 | tf_op jit(solution)/shard_map/all_gather | solution.py:14
  220.3 9.0 %copy.17 = f32[256,64,128]{2,0,1:T(8,128)} copy(f32[256,64,128]{0,2,1:T(8,128)} %bitcast.35) | data formatting | bytes 16777216 | tf_op jit(solution)/shard_map/while | solution.py:47
  229.3 0.1 broadcast_in_dim.24
  229.4 16.8 %while.12 = (s32[]{:T(128)}, f32[256,8,128]{2,1,0:T(8,128)S(1)}, s32[]{:T(128)}, s32[32]{0:T(128)S(1)}, s32[]{:T(128)}, /*index=5*/s32[]{:T(128)}, f32[32,128,12...) while((s32[]{:T(128)}, f32[256,8,128]{2,1,0:T(8,128)S(1)}, ...), condition=%wide.region_1.2_spmd, body=%wide.region_0.1_spmd.sunk | while | flops 428344512 | bytes 9966019 | solution.py:47
  229.4 0.7 compare_and_fusion.2
  230.2 4.0 gather_fusion
  234.2 2.1 convolution_bitcast_fusion.3
  236.3 0.4 copy.22
  236.7 0.1 dynamic-slice_subtract_fusion.2
  236.8 1.0 fusion.23
  237.8 0.7 compare_and_fusion.2
  238.6 4.0 gather_fusion
  242.6 2.1 convolution_bitcast_fusion.3
  244.7 0.4 copy.22
  245.1 0.1 dynamic-slice_subtract_fusion.2
  245.2 1.0 fusion.23
  246.2 1.2 copy.20
  247.4 279.7 %all-reduce.2.cloned.1.call-done = f32[256,1024]{1,0:T(8,128)} async-done(((f32[256,1024]{1,0:T(8,128)}), f32[256,1024]{1,0:T(8,128)}) %all-reduce.2.cloned.1.call-update) | async-done | bytes 1048592 | tf_op jit(solution)/shard_map/psum | solution.py:49
  527.1 1.4 constant_dynamic-slice_fusion
  (11 shorter events, 0.1 us)
Async XLA Ops:
  6.5 138.5 %all-gather.6.cloned.1.call-start = ((), (), s32[]{:S(2)}) async-start(), calls=%async_computation.2 | async-start | bytes 1064960 | tf_op jit(solution)/shard_map/all_gather | solution.py:13
  7.3 204.1 %all-gather.4.cloned.1.call-start = ((), (), s32[]{:S(2)}) async-start(), calls=%async_computation | async-start | bytes 9437184 | tf_op jit(solution)/shard_map/all_gather | solution.py:14
  147.7 379.4 %all-reduce.2.cloned.1.call-start = ((), (), s32[]{:S(2)}) async-start(), calls=%async_computation.1 | async-start | bytes 2097152 | tf_op jit(solution)/shard_map/psum | solution.py:49
  220.3 9.1 %copy-start = (s32[1,1,32]{2,1,0:T(1,128)S(1)}, s32[1,1,32]{2,1,0:T(1,128)}, u32[]{:S(2)}) copy-start(s32[1,1,32]{2,1,0:T(1,128)} %param.10) | copy-start | bytes 388
  220.3 9.1 %copy-start.1 = (s32[1,1,32]{2,1,0:T(1,128)S(1)}, s32[1,1,32]{2,1,0:T(1,128)}, u32[]{:S(2)}) copy-start(s32[1,1,32]{2,1,0:T(1,128)} %param.9) | copy-start | bytes 388
Sparse Core Ops, SparseCore 0:
  10.3 134.7 all-gather.5
  147.9 63.4 all-gather.3
  247.6 279.5 all-reduce.1
where the time goes:
time: 545 us; the launch traced here: 535 us
  waiting for transfers between devices  478 us (88%)
  local copies, waits for them, and re-layouts  35 us (6%)
  between operations  13.8 us (3%)
  matrix products  6.24 us (1%)
    psum x1, waiting for transfers between devices, shards(): summed = lax.psum(partial_sums, 'pair')  280 us
    all_gather x1, waiting for transfers between devices, shards(): gathered_rows = lax.all_gather(t2_amplitudes, 'pair', axis=0, tiled=True)  138 us
    all_gather x1, waiting for transfers between devices, shards(): whole = lax.all_gather(gathered_rows, 'virt', axis=1, tiled=True)  59.9 us
  transfers between devices with their start and end apart: 3, of which 3 were waited for; matrix products, arithmetic and copies ran while one was open for 1% of the time, Pallas kernels for 0%

commit v1 on v0

v1 whole, which is shorter than its diff:
```python
import jax
import jax.numpy as jnp
from jax import lax
from jax.experimental import pallas as pl
from jax.experimental.pallas import tpu as pltpu
from jax.sharding import PartitionSpec as P

W = 128
LIST = 32
NX = 4
NY = 4
NZ = 16
SLOTS = 2 * LIST
MESH = pl.DeviceIdType.MESH
F32 = jnp.float32
I32 = jnp.int32
BF = jnp.bfloat16


def schedule(meta_out, meta_in, counts, sched):
    lane = lax.broadcasted_iota(I32, (W, W), 1)
    sub = lax.broadcasted_iota(I32, (W, W), 0)
    eye = lane == sub
    lane_row = lax.broadcasted_iota(I32, (1, W), 1)
    core = lane_row // LIST
    key_row = jnp.where(lane_row - core * LIST < counts, meta_out, 16)
    key_row = jnp.where(lane_row < SLOTS, key_row, 17)
    keys = jnp.broadcast_to(key_row, (W, W))
    key_col = jnp.sum(jnp.where(eye, keys, 0), axis=1, keepdims=True)
    in_col = jnp.sum(jnp.where(eye, jnp.broadcast_to(meta_in, (W, W)), 0), axis=1, keepdims=True)
    below = jnp.sum((keys < key_col).astype(I32), axis=1, keepdims=True)
    ties = jnp.sum(((keys == key_col) & (lane < sub)).astype(I32), axis=1, keepdims=True)
    rank_col = below + ties
    hot = (rank_col == lane).astype(I32)
    slot_row = jnp.sum(hot * sub, axis=0, keepdims=True)
    in_row = jnp.sum(hot * in_col, axis=0, keepdims=True)
    keep_row = jnp.sum(hot * (ties > 0).astype(I32), axis=0, keepdims=True)
    upto = jnp.sum((key_col <= lane).astype(I32), axis=0, keepdims=True)
    here = jnp.sum((key_col == lane).astype(I32), axis=0, keepdims=True)
    last_row = jnp.where(here > 0, upto - 1, SLOTS)
    sched[0:1, :] = slot_row
    sched[1:2, :] = in_row
    sched[2:3, :] = keep_row
    sched[3:4, :] = last_row


def kernel(
    t2_ref, tiles_ref, outs_ref, ins_ref, count_ref, out_ref,
    rows, stage, slab, tiles, meta, sched, plan, sums, acc,
    rx1, rx2, zsrc, zbuf, zrecv, fin,
    swap_send, swap_recv, tile_send, tile_recv, local_sem, plan_sem,
    zg_send, zg_recv, ex_send, ex_recv, rx_send, rx_recv, zr_send, zr_recv,
):
    pair = lax.axis_index("pair")
    virt = lax.axis_index("virt")
    x, z = pair // NZ, pair % NZ
    y, c = virt // 2, virt % 2
    zr = {"pair": x * NZ + (z + 1) % NZ, "virt": virt}
    zl = {"pair": x * NZ + (z + NZ - 1) % NZ, "virt": virt}
    xr = {"pair": (x + 1) % NX * NZ + z, "virt": virt}
    xl = {"pair": (x + NX - 1) % NX * NZ + z, "virt": virt}
    yr = {"pair": pair, "virt": (y + 1) % NY * 2 + c}
    yl = {"pair": pair, "virt": (y + NY - 1) % NY * 2 + c}
    mate = {"pair": pair, "virt": y * 2 + 1 - c}

    def copy(src, dst, send, recv, device):
        return pltpu.make_async_remote_copy(
            src_ref=src, dst_ref=dst, send_sem=send, recv_sem=recv, device_id=device, device_id_type=MESH
        )

    barrier = pltpu.get_barrier_semaphore()
    for peer in (zr, zl, xr, xl, yr, yl, mate):
        pl.semaphore_signal(barrier, inc=1, device_id=peer, device_id_type=MESH)

    for row in range(4):
        for j in range(8):
            at = (row % 2) * 8 + j
            rows[row // 2, at : at + 1, :] = t2_ref[row : row + 1, j * W : (j + 1) * W]
    base = pl.multiple_of(z * 32, 32)
    mine = pl.multiple_of(c * 8, 8)
    for r in range(2):
        stage[pl.ds(base + r * 16 + mine, 8), :] = rows[c, r * 8 : r * 8 + 8, :]
    pad = jnp.zeros((1, W - LIST), I32)
    first = virt // 2 * 16
    meta[c, 0:1, :] = jnp.concatenate([outs_ref[0] - first, pad], axis=1)
    meta[c, 1:2, :] = jnp.concatenate([ins_ref[0], pad], axis=1)
    meta[c, 2:3, :] = jnp.broadcast_to(count_ref[0:1, 0:1], (1, W))
    pl.semaphore_wait(barrier, 7)

    swaps = []
    for r in range(2):
        part = stage.at[pl.ds(base + r * 16 + mine, 8), :]
        swaps.append(copy(rows.at[1 - c, pl.ds(r * 8, 8), :], part, swap_send.at[r], swap_recv.at[r], mate))
    swaps.append(copy(meta.at[c], meta.at[c], swap_send.at[2], swap_recv.at[2], mate))
    for one in swaps:
        one.start()
    theirs = pl.multiple_of((1 - c) * 8, 8)
    for r in range(2):
        part = stage.at[pl.ds(base + r * 16 + theirs, 8), :]
        copy(rows.at[1 - c, pl.ds(r * 8, 8), :], part, swap_send.at[r], swap_recv.at[r], mate).wait_recv()

    def chunk(q):
        return stage.at[pl.ds(pl.multiple_of(q % NZ * 32, 32), 32), :]

    def z_right(step, origin):
        return copy(chunk(origin), chunk(origin), zg_send.at[0, step], zg_recv.at[0, step], zr)

    def z_left(step, origin):
        return copy(chunk(origin), chunk(origin), zg_send.at[1, step], zg_recv.at[1, step], zl)

    for step in range(8):
        z_right(step, z + NZ - step).start()
        if step < 7:
            z_left(step, z + step).start()
        if step == 0:
            local = pltpu.make_async_copy(tiles_ref, tiles.at[pl.ds(c * LIST, LIST)], local_sem)
            local.start()
            across = copy(tiles_ref, tiles.at[pl.ds(c * LIST, LIST)], tile_send, tile_recv, mate)
            across.start()
        z_right(step, z + 2 * NZ - 1 - step).wait_recv()
        if step < 7:
            z_left(step, z + 1 + step).wait_recv()

    here = pl.multiple_of(x * 32, 32)

    def relayout(t, _):
        for r in range(2):
            slab[y, t, pl.ds(here + r * 16, 16), :] = stage[pl.ds(r * 16 + t, 16, stride=32), :]
        return 0

    lax.fori_loop(0, 16, relayout, 0)

    def x_rows(q):
        return pl.ds(pl.multiple_of(q * 32, 32), 32)

    def sel_0(h, q):
        return slab.at[y, pl.ds(4 * h, 4), x_rows(q), :]

    def sel_1(h, q):
        return slab.at[q, pl.ds(8 + 4 * h, 4), x_rows(x), :]

    def sel_2(h, q):
        return slab.at[q, pl.ds(4 * h, 4), :, :]

    def sel_3(h, q):
        return slab.at[:, pl.ds(8 + 4 * h, 4), x_rows(q), :]

    sels = (sel_0, sel_1, sel_2, sel_3)
    spots = (x, y, y, x)
    rights = (xr, yr, yr, xr)
    lefts = (xl, yl, yl, xl)

    def ex(n, k, h, q, device):
        ref = sels[n](h, q)
        return copy(ref, ref, ex_send.at[n, k], ex_recv.at[n, k], device)

    def sent(n, k):
        q = spots[n]
        q = (q, q, q, q, (q + 3) % 4, (q + 1) % 4)[k]
        return ex(n, k, (0, 1, 1, 0, 0, 1)[k], q, (rights, lefts)[k % 2][n])

    def got(n, k):
        q = spots[n]
        before, after, far = (q + 3) % 4, (q + 1) % 4, (q + 2) % 4
        q = (before, after, before, after, far, far)[k]
        return ex(n, k, (0, 1, 1, 0, 0, 1)[k], q, (rights, lefts)[k % 2][n])

    def run(pairs, between):
        for k in range(4):
            for n in pairs:
                sent(n, k).start()
        between()
        for k in range(2):
            for n in pairs:
                got(n, k).wait_recv()
                sent(n, 4 + k).start()
        for k in range(2, 6):
            for n in pairs:
                got(n, k).wait_recv()

    def prepare():
        copy(meta.at[c], meta.at[1 - c], swap_send.at[2], swap_recv.at[2], mate).wait_recv()
        low = lax.broadcasted_iota(I32, (1, W), 1) < LIST
        both = [
            jnp.where(low, meta[0, k : k + 1, :], pltpu.roll(meta[1, k : k + 1, :], LIST, 1)) for k in range(3)
        ]
        schedule(both[0], both[1], both[2], sched)
        turn = pltpu.make_async_copy(sched, plan, plan_sem)
        turn.start()
        turn.wait()

    run((0, 1), lambda: None)
    run((2, 3), prepare)
    local.wait()
    copy(tiles_ref, tiles.at[pl.ds((1 - c) * LIST, LIST)], tile_send, tile_recv, mate).wait_recv()

    sums[SLOTS] = jnp.zeros((W, W), F32)

    def slot(k, total):
        a = slab[plan[1, k] // 16, plan[1, k] % 16]
        b = tiles[plan[0, k]]
        keep = plan[2, k].astype(F32)
        a_high = a.astype(BF)
        a_low = (a - a_high.astype(F32)).astype(BF)
        b_high = b.astype(BF)
        b_low = (b - b_high.astype(F32)).astype(BF)
        left = jnp.concatenate([a_high, a_low], axis=1)
        right = jnp.concatenate([b_high, b_low], axis=1)
        right = jnp.concatenate([right, right], axis=0)
        product = jnp.dot(left, right, preferred_element_type=F32)
        total = total * keep + (product[:, :W] + product[:, W:])
        sums[k] = total
        return total

    lax.fori_loop(0, SLOTS, slot, jnp.zeros((W, W), F32))

    def pick(t, _):
        acc[t] = sums[plan[3, t]]
        return 0

    lax.fori_loop(0, 16, pick, 0)

    right_x, left_x, far_x = (x + 1) % NX, (x + 3) % NX, (x + 2) % NX

    def lot(lo, size, q):
        return acc.at[pl.ds(lo, size), x_rows(q), :]

    sums_x = [
        copy(lot(0, 8, far_x), rx1.at[0], rx_send.at[0], rx_recv.at[0], xr),
        copy(lot(8, 8, far_x), rx1.at[1], rx_send.at[1], rx_recv.at[1], xl),
        copy(lot(8, 8, right_x), rx2.at[0, pl.ds(8, 8)], rx_send.at[2], rx_recv.at[2], xr),
        copy(lot(0, 8, left_x), rx2.at[1, pl.ds(0, 8)], rx_send.at[3], rx_recv.at[3], xl),
        copy(lot(0, 8, right_x), rx2.at[0, pl.ds(0, 8)], rx_send.at[4], rx_recv.at[4], xr),
        copy(lot(8, 8, left_x), rx2.at[1, pl.ds(8, 8)], rx_send.at[5], rx_recv.at[5], xl),
    ]
    for one in sums_x[:4]:
        one.start()
    sums_x[0].wait_recv()

    def add_right(t, _):
        acc[t, x_rows(right_x), :] += rx1[0, t]
        return 0

    lax.fori_loop(0, 8, add_right, 0)
    sums_x[4].start()
    sums_x[1].wait_recv()

    def add_left(t, _):
        acc[8 + t, x_rows(left_x), :] += rx1[1, t]
        return 0

    lax.fori_loop(0, 8, add_left, 0)
    sums_x[5].start()
    for one in sums_x[2:]:
        one.wait_recv()

    def add_here(t, _):
        zsrc[pl.ds(pl.multiple_of(t * 32, 32), 32), :] = acc[t, x_rows(x), :] + rx2[0, t] + rx2[1, t]
        return 0

    lax.fori_loop(0, 16, add_here, 0)

    def split(q, _):
        for r in range(2):
            zbuf[q, r * 16 : r * 16 + 16, :] = zsrc[pl.ds(r * 16 + q, 16, stride=32), :]
        return 0

    lax.fori_loop(0, NZ, split, 0)

    def sum_right(step):
        q = (z + NZ + 8 - step) % NZ
        return copy(zbuf.at[q], zrecv.at[0, step], zr_send.at[0, step], zr_recv.at[0, step], zr)

    def sum_left(step):
        q = (z + NZ - 7 + step) % NZ
        return copy(zbuf.at[q], zrecv.at[1, step], zr_send.at[1, step], zr_recv.at[1, step], zl)

    for step in range(8):
        if step > 0:
            sum_right(step - 1).wait_recv()
            q = (z + NZ + 8 - step) % NZ
            zbuf[q] += zrecv[0, step - 1]
        sum_right(step).start()
        if step < 7:
            if step > 0:
                sum_left(step - 1).wait_recv()
                q = (z + NZ - 7 + step) % NZ
                zbuf[q] += zrecv[1, step - 1]
            sum_left(step).start()
    sum_right(7).wait_recv()
    sum_left(6).wait_recv()
    zbuf[z] += zrecv[0, 7] + zrecv[1, 6]

    for r in range(2):
        fin[c, r * 8 : r * 8 + 8, :] = zbuf[z, pl.ds(r * 16 + mine, 8), :]
    last = [
        copy(zbuf.at[z, pl.ds(r * 16 + theirs, 8), :], fin.at[c, pl.ds(r * 8, 8), :], swap_send.at[3 + r], swap_recv.at[3 + r], mate)
        for r in range(2)
    ]
    for one in last:
        one.start()
    for r in range(2):
        copy(zbuf.at[z, pl.ds(r * 16 + theirs, 8), :], fin.at[1 - c, pl.ds(r * 8, 8), :], swap_send.at[3 + r], swap_recv.at[3 + r], mate).wait_recv()
    for row in range(4):
        for j in range(8):
            at = (row % 2) * 8 + j
            out_ref[row : row + 1, j * W : (j + 1) * W] = fin[row // 2, at : at + 1, :]

    for one in swaps + last + sums_x:
        one.wait_send()
    across.wait_send()
    for step in range(8):
        z_right(step, z + NZ - step).wait_send()
        sum_right(step).wait_send()
        if step < 7:
            z_left(step, z + step).wait_send()
            sum_left(step).wait_send()
    for n in range(4):
        for k in range(6):
            sent(n, k).wait_send()


def shards(t2_amplitudes, integral_tiles, out_tiles, in_tiles, tile_counts):
    vmem = pl.BlockSpec(memory_space=pltpu.VMEM)
    dma = pltpu.SemaphoreType.DMA
    return pl.pallas_call(
        kernel,
        out_shape=jax.ShapeDtypeStruct(t2_amplitudes.shape, F32),
        in_specs=[vmem, pl.BlockSpec(memory_space=pltpu.HBM), vmem, vmem, vmem],
        out_specs=vmem,
        scratch_shapes=[
            pltpu.VMEM((2, 16, W), F32),
            pltpu.VMEM((NZ * 32, W), F32),
            pltpu.VMEM((NY, 16, W, W), F32),
            pltpu.VMEM((SLOTS, W, W), F32),
            pltpu.VMEM((2, 8, W), I32),
            pltpu.VMEM((8, W), I32),
            pltpu.SMEM((8, W), I32),
            pltpu.VMEM((SLOTS + 1, W, W), F32),
            pltpu.VMEM((16, W, W), F32),
            pltpu.VMEM((2, 8, 32, W), F32),
            pltpu.VMEM((2, 16, 32, W), F32),
            pltpu.VMEM((16 * 32, W), F32),
            pltpu.VMEM((NZ, 32, W), F32),
            pltpu.VMEM((2, 8, 32, W), F32),
            pltpu.VMEM((2, 16, W), F32),
            dma((5,)), dma((5,)), dma, dma, dma, dma,
            dma((2, 8)), dma((2, 8)), dma((4, 6)), dma((4, 6)), dma((6,)), dma((6,)), dma((2, 8)), dma((2, 8)),
        ],
        compiler_params=pltpu.CompilerParams(
            collective_id=0, has_side_effects=True, vmem_limit_bytes=48 * 1024 * 1024
        ),
    )(t2_amplitudes, integral_tiles.reshape(LIST, W, W), out_tiles, in_tiles, tile_counts)


def solution(mesh):
    return jax.shard_map(
        shards,
        mesh=mesh,
        in_specs=(
            P("pair", "virt"),
            P("pair", "virt", None, None, None),
            P("pair", "virt", None),
            P("pair", "virt", None),
            P("pair", "virt"),
        ),
        out_specs=P("pair", "virt"),
        check_vma=False,
    )
```

time: 545 us -> 113 us (0.21); the launches traced: 535 us -> 113 us
  waiting for transfers between devices: 478 us -> 0 us
  Pallas kernels: 0 us -> 108 us
  local copies, waits for them, and re-layouts: 35 us -> 4.22 us
  between operations: 13.8 us -> 0.67 us
  matrix products: 6.24 us -> 0 us
    psum x1 -> x0, waiting for transfers between devices: 280 us -> none  [shards(): summed = lax.psum(partial_sums, 'pair')]
    all_gather x2 -> x0, waiting for transfers between devices: 198 us -> none  [the longest x1 138 us: shards(): gathered_rows = lax.all_gather(t2_amplitudes, 'pair', axis=0, tiled=True)]
    pallas_call x0 -> x1, Pallas kernels: none -> 108 us  [shards(): pl.pallas_call(kernel, out_shape=jax.ShapeDtypeStruct(t2_amplitudes.shape...]
    while x1 -> x0, local copies, waits for them, and re-layouts: 9.02 us -> none  [shards(): totals = lax.fori_loop(0, group_steps, one_group, start_totals)]
    all_gather x1 -> x0, local copies, waits for them, and re-layouts: 8.98 us -> none  [shards(): whole = lax.all_gather(gathered_rows, 'virt', axis=1, tiled=True)]
    gather x2 -> x0, local copies, waits for them, and re-layouts: 7.99 us -> none  [one_group(): columns = jnp.take(blocks, ins, axis=1)]
    dot_general x4 -> x0, matrix products: 6.24 us -> none  [the longest x2 4.3 us: one_group(): jnp.einsum('psc,sca->psa', columns, group_tiles_now, precision=lax.Precis...]
  transfers between devices with their start and end apart: 3 -> 0, of which waited for: 3 -> 0; matrix products, arithmetic and copies ran while one was open for 1% -> 0% of each run, Pallas kernels for 0% -> 0%
where the time goes in v1:
time: 113 us
  Pallas kernels  108 us (96%)
  local copies, waits for them, and re-layouts  4.22 us (4%)
    pallas_call x1, Pallas kernels, shards(): pl.pallas_call(kernel, out_shape=jax.ShapeDtypeStruct(t2_amplitudes.shape...  108 us
    unnamed x9, local copies, waits for them, and re-layouts  4.22 us

profile of v1, /device:TPU:1, one launch (start us, length us, event | category | flops | bytes accessed | tf_op | source)
XLA Modules:
  0.0 113.1 jit_solution(6052036272685774022)
XLA Ops:
  0.7 0.0 copy-start
  0.7 1.6 %copy-done = f32[1,1,32,128,128]{4,3,2,1,0:T(8,128)S(1)} copy-done((f32[1,1,32,128,128]{4,3,2,1,0:T(8,128)S(1)}, f32[1,1,32,128,128]{4,3,2,1,0:T(8,128)}, u32[]{:S(2)}) %copy-start) | copy-done | bytes 2097176
  2.2 0.0 copy-start.1
  2.2 0.7 copy-done.1
  3.0 0.0 copy-start.2
  3.0 0.7 copy-done.2
  3.6 0.0 copy-start.3
  3.6 0.7 copy-done.3
  4.3 108.2 %shard_map.55 = f32[4,1024]{1,0:T(4,128)S(1)} custom-call(f32[4,1024]{1,0:T(4,128)S(1)} %copy-done.1, f32[32,128,128]{2,1,0:T(8,128)S(1)} %bitcast.1, s32[1,1,32]{2,1,0:T(1,128)S(1)} %copy-done.2, s32[1,1,32]{2,1,0:T(1,128)S(1)} %copy-done.3, s32[1,1]{1,0:T(1,128)S(6)} %copy.7.count_ref), custom_call_target="tpu_custom_call" | custom-call | tf_op jit(solution)/shard_map/pallas_call | solution.py:326
  112.4 0.6 copy.8
Async XLA Ops:
  0.7 1.6 %copy-start = (f32[1,1,32,128,128]{4,3,2,1,0:T(8,128)S(1)}, f32[1,1,32,128,128]{4,3,2,1,0:T(8,128)}, u32[]{:S(2)}) copy-start(f32[1,1,32,128,128]{4,3,2,1,0:T(8,128)} %param.6) | copy-start | bytes 6291460
  2.2 0.7 copy-start.1
  3.0 0.7 copy-start.2
  3.6 0.7 copy-start.3

commit v2 on v0

v2 whole, which is shorter than its diff:
```python
import jax
import jax.numpy as jnp
from jax import lax
from jax.experimental import pallas as pl
from jax.experimental.pallas import tpu as pltpu
from jax.sharding import PartitionSpec as P

W = 128
LIST = 32
NX = 4
NY = 4
NZ = 16
SLOTS = 2 * LIST
MESH = pl.DeviceIdType.MESH
F32 = jnp.float32
I32 = jnp.int32
BF = jnp.bfloat16
DELTAS = (0, 1, -1, 2, -2, 3, -3, 4, -4, 5, -5, 6, -6, 7, -7, 8)
SLOT_OF = {d: i for i, d in enumerate(DELTAS)}
SLOT_OF[-8] = SLOT_OF[8]
GROUPS = ((0, 9), (9, 16))


def schedule(key_row, in_row, sched):
    lane = lax.broadcasted_iota(I32, (W, W), 1)
    sub = lax.broadcasted_iota(I32, (W, W), 0)
    eye = lane == sub
    keys = jnp.broadcast_to(key_row, (W, W))
    key_col = jnp.sum(jnp.where(eye, keys, 0), axis=1, keepdims=True)
    in_col = jnp.sum(jnp.where(eye, jnp.broadcast_to(in_row, (W, W)), 0), axis=1, keepdims=True)
    below = jnp.sum((keys < key_col).astype(I32), axis=1, keepdims=True)
    ties = jnp.sum(((keys == key_col) & (lane < sub)).astype(I32), axis=1, keepdims=True)
    hot = ((below + ties) == lane).astype(I32)
    tile = lane + lane // 8
    upto = jnp.sum((key_col <= tile).astype(I32), axis=0, keepdims=True)
    here = jnp.sum((key_col == tile).astype(I32), axis=0, keepdims=True)
    sched[0:1, :] = jnp.sum(hot * sub, axis=0, keepdims=True)
    sched[1:2, :] = jnp.sum(hot * in_col, axis=0, keepdims=True)
    sched[2:3, :] = jnp.sum(hot * (ties > 0).astype(I32), axis=0, keepdims=True)
    sched[3:4, :] = jnp.where(here > 0, upto - 1, SLOTS)


def kernel(
    t2_ref, tiles_ref, outs_ref, ins_ref, count_ref, out_ref,
    rows, stage, tiles, halves, meta, sched, plan, sums, acc, rx, zbuf, zrx, total, fin,
    swap_send, swap_recv, local_sem, plan_sem,
    zg_send, zg_recv, p1_send, p1_recv, p2_send, p2_recv, rx_send, rx_recv, zr_send, zr_recv,
):
    pair = lax.axis_index("pair")
    virt = lax.axis_index("virt")
    x, z = pair // NZ, pair % NZ
    y, c = virt // 2, virt % 2

    def at_z(d):
        return {"pair": x * NZ + (z + d + NZ) % NZ, "virt": virt}

    def at_x(d):
        return {"pair": (x + d) % NX * NZ + z, "virt": virt}

    def at_y(d):
        return {"pair": pair, "virt": (y + d) % NY * 2 + c}

    mate = {"pair": pair, "virt": y * 2 + 1 - c}

    def copy(src, dst, send, recv, device):
        return pltpu.make_async_remote_copy(
            src_ref=src, dst_ref=dst, send_sem=send, recv_sem=recv, device_id=device, device_id_type=MESH
        )

    sent = []

    def start(*what):
        one = copy(*what)
        one.start()
        sent.append(one)

    def arrived(ref, send, recv):
        copy(ref, ref, send, recv, mate).wait_recv()

    barrier = pltpu.get_barrier_semaphore()
    peers = [mate] + [at_z(d) for k in (4, 3, 2, 1) for d in (k, -k)]
    peers += [at_x(d) for d in (2, 1, 3)] + [at_y(d) for d in (2, 1, 3)]
    for peer in peers:
        pl.semaphore_signal(barrier, inc=1, device_id=peer, device_id_type=MESH)

    for row in range(4):
        for j in range(8):
            at = (row % 2) * 8 + j
            rows[row // 2, at : at + 1, :] = t2_ref[row : row + 1, j * W : (j + 1) * W]
    stage[c, 0, 0, 0] = rows[c]
    local = pltpu.make_async_copy(tiles_ref, tiles.at[pl.ds(c * LIST, LIST)], local_sem)
    local.start()
    lane = lax.broadcasted_iota(I32, (1, W), 1)
    pad = jnp.zeros((1, W - LIST), I32)
    key = jnp.concatenate([outs_ref[0] - y * 16, pad], axis=1) - c * 8
    key = jnp.where(lane < count_ref[0:1, 0:1], key, 8) + c * 9
    meta[c, 0:1, :] = key
    meta[c, 1:2, :] = jnp.concatenate([ins_ref[0], pad], axis=1)
    sums[SLOTS] = jnp.zeros((W, W), F32)
    pl.semaphore_wait(barrier, len(peers))

    start(rows.at[1 - c], stage.at[c, 0, 0, 0], swap_send.at[0], swap_recv.at[0], mate)
    start(meta.at[c], meta.at[c], swap_send.at[1], swap_recv.at[1], mate)
    arrived(stage.at[1 - c, 0, 0, 0], swap_send.at[0], swap_recv.at[0])

    def z_chunk(slot):
        return stage.at[:, 0, 0, slot]

    def z_start(slot, d):
        at = SLOT_OF[DELTAS[slot] - d]
        start(z_chunk(slot), z_chunk(at), zg_send.at[at], zg_recv.at[at], at_z(d))

    def z_arrived(slot):
        arrived(z_chunk(slot), zg_send.at[slot], zg_recv.at[slot])

    for k in (4, 3, 2, 1):
        z_start(0, k)
        z_start(0, -k)
    start(tiles_ref, tiles.at[pl.ds(c * LIST, LIST)], swap_send.at[2], swap_recv.at[2], mate)
    for k in (1, 2, 3, 4):
        z_arrived(SLOT_OF[-k])
        z_start(SLOT_OF[-k], 4)
        z_arrived(SLOT_OF[k])
        if k < 4:
            z_start(SLOT_OF[k], -4)

    def first_at(h, g, at):
        a, b = GROUPS[g]
        return stage.at[0, 0, at, pl.ds(a, b - a)] if h == 0 else stage.at[1, at, 0, pl.ds(a, b - a)]

    def first_start(g):
        for d in (2, 1, 3):
            for h in range(2):
                sems = p1_send.at[h, g, d - 1], p1_recv.at[h, g, d - 1]
                start(first_at(h, g, 0), first_at(h, g, 4 - d), *sems, (at_x, at_y)[h](d))

    def first_arrived(g):
        for d in (1, 3, 2):
            for h in range(2):
                arrived(first_at(h, g, 4 - d), p1_send.at[h, g, d - 1], p1_recv.at[h, g, d - 1])

    def second_at(h, g, at, part):
        a, b = GROUPS[g]
        if h == 0:
            return stage.at[0, at, pl.ds(2 * part, 2), pl.ds(a, b - a)]
        return stage.at[1, pl.ds(2 * part, 2), at, pl.ds(a, b - a)]

    MOVES = ((0, 0, 1), (0, 1, 3), (0, 1, 1), (0, 0, 3), (3, 0, 1), (1, 1, 3))

    def second_start(g, k):
        at, part, d = MOVES[k]
        for h in range(2):
            sems = p2_send.at[h, g, k], p2_recv.at[h, g, k]
            start(second_at(h, g, at, part), second_at(h, g, (at + 4 - d) % 4, part), *sems, (at_y, at_x)[h](d))

    def second_arrived(g, k):
        at, part, d = MOVES[k]
        for h in range(2):
            arrived(second_at(h, g, (at + 4 - d) % 4, part), p2_send.at[h, g, k], p2_recv.at[h, g, k])

    first_start(0)

    arrived(meta.at[1 - c], swap_send.at[1], swap_recv.at[1])
    low = lane < LIST
    both = [jnp.where(low, meta[0, k : k + 1, :], pltpu.roll(meta[1, k : k + 1, :], LIST, 1)) for k in range(2)]
    schedule(jnp.where(lane < SLOTS, both[0], 18), both[1], sched)
    turn = pltpu.make_async_copy(sched, plan, plan_sem)
    turn.start()
    local.wait()
    arrived(tiles.at[pl.ds((1 - c) * LIST, LIST)], swap_send.at[2], swap_recv.at[2])

    def halve(s, _):
        b = tiles[s]
        high = b.astype(BF)
        halves[s, :, :W] = high
        halves[s, :, W:] = (b - high.astype(F32)).astype(BF)
        return 0

    lax.fori_loop(0, SLOTS, halve, 0, unroll=4)
    turn.wait()

    first_arrived(0)
    for k in range(4):
        second_start(0, k)
    for k in (1, 2, 3, 4):
        z_arrived(SLOT_OF[-4 - k])
        if k < 4:
            z_arrived(SLOT_OF[4 + k])
    first_start(1)
    for k in (0, 1):
        second_arrived(0, k)
        second_start(0, 4 + k)
    first_arrived(1)
    for k in range(4):
        second_start(1, k)
    for k in range(2, 6):
        second_arrived(0, k)
    for k in (0, 1):
        second_arrived(1, k)
        second_start(1, 4 + k)
    for k in range(2, 6):
        second_arrived(1, k)

    flat = stage.reshape(2 * 4 * 4 * 16 * 16, W)

    def slot(k, running):
        n = plan[1, k]
        dy = (n // 16 + 4 - y) % 4
        a = flat[pl.ds((n // 8 % 2 * 4 + dy) * 1024 + n % 8, W, stride=8), :]
        keep = plan[2, k].astype(F32)
        high = a.astype(BF)
        a = jnp.concatenate([high, (a - high.astype(F32)).astype(BF)], axis=1)
        b = halves[plan[0, k]]
        product = jnp.dot(a, jnp.concatenate([b, b], axis=0), preferred_element_type=F32)
        running = running * keep + (product[:, :W] + product[:, W:])
        sums[k] = running
        return running

    def x_part(h, d):
        return acc.at[pl.ds(h * 8, 8), pl.ds(d * 32, 32), :]

    for h in range(2):
        lax.fori_loop(h * LIST, h * LIST + LIST, slot, jnp.zeros((W, W), F32), unroll=4)

        def pick(t, _):
            acc[t] = sums[plan[3, t]]
            return 0

        lax.fori_loop(h * 8, h * 8 + 8, pick, 0)
        for d in (2, 1, 3):
            start(x_part(h, d), rx.at[h, 3 - d], rx_send.at[h, 3 - d], rx_recv.at[h, 3 - d], at_x(d))

    acc_rows = acc.reshape(16 * W, W)
    rx_rows = rx.reshape(2 * 3 * 8 * 32, W)
    for h in range(2):
        for i in range(3):
            arrived(rx.at[h, i], rx_send.at[h, i], rx_recv.at[h, i])

        def add(s, _):
            for r in range(2):
                at = s * 2 + r
                value = acc_rows[pl.ds(h * 8 * W + at, 8, stride=W), :]
                for i in range(3):
                    value += rx_rows[pl.ds((h * 3 + i) * 256 + at, 8, stride=32), :]
                zbuf[h, s, r * 8 : r * 8 + 8, :] = value
            return 0

        lax.fori_loop(0, NZ, add, 0, unroll=2)
        for s in range(NZ - 1, 0, -1):
            back = SLOT_OF[-DELTAS[s]]
            start(zbuf.at[h, s], zrx.at[h, back], zr_send.at[h, back], zr_recv.at[h, back], at_z(DELTAS[s]))

    for h in range(2):
        value = zbuf[h, 0]
        for s in range(1, NZ):
            arrived(zrx.at[h, s], zr_send.at[h, s], zr_recv.at[h, s])
            value += zrx[h, s]
        total[h] = value

    fin[c] = total[c]
    start(total.at[1 - c], fin.at[c], swap_send.at[3], swap_recv.at[3], mate)
    arrived(fin.at[1 - c], swap_send.at[3], swap_recv.at[3])
    for row in range(4):
        for j in range(8):
            at = (row % 2) * 8 + j
            out_ref[row : row + 1, j * W : (j + 1) * W] = fin[row // 2, at : at + 1, :]

    for one in sent:
        one.wait_send()


def shards(t2_amplitudes, integral_tiles, out_tiles, in_tiles, tile_counts):
    vmem = pl.BlockSpec(memory_space=pltpu.VMEM)
    dma = pltpu.SemaphoreType.DMA
    return pl.pallas_call(
        kernel,
        out_shape=jax.ShapeDtypeStruct(t2_amplitudes.shape, F32),
        in_specs=[vmem, pl.BlockSpec(memory_space=pltpu.HBM), vmem, vmem, vmem],
        out_specs=vmem,
        scratch_shapes=[
            pltpu.VMEM((2, 16, W), F32),
            pltpu.VMEM((2, NY, NX, NZ, 16, W), F32),
            pltpu.VMEM((SLOTS, W, W), F32),
            pltpu.VMEM((SLOTS, W, 2 * W), BF),
            pltpu.VMEM((2, 8, W), I32),
            pltpu.VMEM((8, W), I32),
            pltpu.SMEM((8, W), I32),
            pltpu.VMEM((SLOTS + 1, W, W), F32),
            pltpu.VMEM((16, W, W), F32),
            pltpu.VMEM((2, 3, 8, 32, W), F32),
            pltpu.VMEM((2, NZ, 16, W), F32),
            pltpu.VMEM((2, NZ, 16, W), F32),
            pltpu.VMEM((2, 16, W), F32),
            pltpu.VMEM((2, 16, W), F32),
            dma((4,)), dma((4,)), dma, dma,
            dma((NZ,)), dma((NZ,)), dma((2, 2, 3)), dma((2, 2, 3)), dma((2, 2, 6)), dma((2, 2, 6)),
            dma((2, 3)), dma((2, 3)), dma((2, NZ)), dma((2, NZ)),
        ],
        compiler_params=pltpu.CompilerParams(
            collective_id=0, has_side_effects=True, vmem_limit_bytes=62 * 1024 * 1024
        ),
    )(t2_amplitudes, integral_tiles.reshape(LIST, W, W), out_tiles, in_tiles, tile_counts)


def solution(mesh):
    return jax.shard_map(
        shards,
        mesh=mesh,
        in_specs=(
            P("pair", "virt"),
            P("pair", "virt", None, None, None),
            P("pair", "virt", None),
            P("pair", "virt", None),
            P("pair", "virt"),
        ),
        out_specs=P("pair", "virt"),
        check_vma=False,
    )
```

time: 545 us -> 80.1 us (0.15); the launches traced: 535 us -> 79.8 us
  waiting for transfers between devices: 478 us -> 0 us
  Pallas kernels: 0 us -> 77.9 us
  local copies, waits for them, and re-layouts: 35 us -> 1.32 us
  between operations: 13.8 us -> 0.66 us
  matrix products: 6.24 us -> 0 us
    psum x1 -> x0, waiting for transfers between devices: 280 us -> none  [shards(): summed = lax.psum(partial_sums, 'pair')]
    all_gather x2 -> x0, waiting for transfers between devices: 198 us -> none  [the longest x1 138 us: shards(): gathered_rows = lax.all_gather(t2_amplitudes, 'pair', axis=0, tiled=True)]
    pallas_call x0 -> x1, Pallas kernels: none -> 77.9 us  [shards(): pl.pallas_call(kernel, out_shape=jax.ShapeDtypeStruct(t2_amplitudes.shape...]
    while x1 -> x0, local copies, waits for them, and re-layouts: 9.02 us -> none  [shards(): totals = lax.fori_loop(0, group_steps, one_group, start_totals)]
    all_gather x1 -> x0, local copies, waits for them, and re-layouts: 8.98 us -> none  [shards(): whole = lax.all_gather(gathered_rows, 'virt', axis=1, tiled=True)]
    gather x2 -> x0, local copies, waits for them, and re-layouts: 7.99 us -> none  [one_group(): columns = jnp.take(blocks, ins, axis=1)]
    dot_general x4 -> x0, matrix products: 6.24 us -> none  [the longest x2 4.3 us: one_group(): jnp.einsum('psc,sca->psa', columns, group_tiles_now, precision=lax.Precis...]
    unnamed x7 -> x1, local copies, waits for them, and re-layouts: 6.8 us -> 1.32 us
  transfers between devices with their start and end apart: 3 -> 0, of which waited for: 3 -> 0; matrix products, arithmetic and copies ran while one was open for 1% -> 0% of each run, Pallas kernels for 0% -> 0%
where the time goes in v2:
time: 80.1 us; the launch traced here: 79.8 us
  Pallas kernels  77.9 us (97%)
  local copies, waits for them, and re-layouts  1.32 us (2%)
    pallas_call x1, Pallas kernels, shards(): pl.pallas_call(kernel, out_shape=jax.ShapeDtypeStruct(t2_amplitudes.shape...  77.9 us

profile of v2, /device:TPU:1, one launch (start us, length us, event | category | flops | bytes accessed | tf_op | source)
XLA Modules:
  0.0 79.8 jit_solution(9513798791164575453)
XLA Ops:
  0.7 77.9 %shard_map.55 = f32[4,1024]{1,0:T(4,128)} custom-call(f32[4,1024]{1,0:T(4,128)} %t2_ref.1, f32[32,128,128]{2,1,0:T(8,128)} %bitcast.1, s32[1,1,32]{2,1,0:T(1,128)} %outs_ref.1, s32[1,1,32]{2,1,0:T(1,128)} %ins_ref.1, s32[1,1]{1,0:T(1,128)S(6)} %copy.7.count_ref), custom_call_target="tpu_custom_call" | custom-call | tf_op jit(solution)/shard_map/pallas_call | solution.py:275
  78.5 1.3 %copy.8 = f32[4,1024]{1,0:T(4,128)} copy(f32[4,1024]{1,0:T(4,128)} %shard_map.55) | data formatting | bytes 32768

commit v3 on v2

v3 whole, which is shorter than its diff:
```python
import jax
import jax.numpy as jnp
from jax import lax
from jax.experimental import pallas as pl
from jax.experimental.pallas import tpu as pltpu
from jax.sharding import PartitionSpec as P

W = 128
LIST = 32
NX = 4
NY = 4
NZ = 16
SLOTS = 2 * LIST
MESH = pl.DeviceIdType.MESH
F32 = jnp.float32
I32 = jnp.int32
BF = jnp.bfloat16
DELTAS = (0, 1, -1, 2, -2, 3, -3, 4, -4, 5, -5, 6, -6, 7, -7, 8)
SLOT_OF = {d: i for i, d in enumerate(DELTAS)}
SLOT_OF[-8] = SLOT_OF[8]
GROUPS = ((0, 1), (3, 5), (5, 8), (8, 13), (13, 16))
NG = len(GROUPS)


def schedule(key_row, in_row, sched):
    lane = lax.broadcasted_iota(I32, (W, W), 1)
    sub = lax.broadcasted_iota(I32, (W, W), 0)
    eye = lane == sub
    keys = jnp.broadcast_to(key_row, (W, W))
    key_col = jnp.sum(jnp.where(eye, keys, 0), axis=1, keepdims=True)
    in_col = jnp.sum(jnp.where(eye, jnp.broadcast_to(in_row, (W, W)), 0), axis=1, keepdims=True)
    below = jnp.sum((keys < key_col).astype(I32), axis=1, keepdims=True)
    ties = jnp.sum(((keys == key_col) & (lane < sub)).astype(I32), axis=1, keepdims=True)
    hot = ((below + ties) == lane).astype(I32)
    tile = lane + lane // 8
    upto = jnp.sum((key_col <= tile).astype(I32), axis=0, keepdims=True)
    here = jnp.sum((key_col == tile).astype(I32), axis=0, keepdims=True)
    sched[0:1, :] = jnp.sum(hot * sub, axis=0, keepdims=True)
    sched[1:2, :] = jnp.sum(hot * in_col, axis=0, keepdims=True)
    sched[2:3, :] = jnp.sum(hot * (ties > 0).astype(I32), axis=0, keepdims=True)
    sched[3:4, :] = jnp.where(here > 0, upto - 1, SLOTS)


def kernel(
    t2_hbm, tiles_ref, outs_hbm, ins_hbm, count_ref, out_ref,
    t2_ref, outs_ref, ins_ref, rows, stage_a, stage_b, tiles, halves, meta, sched, plan, sums, acc, rx, zbuf, zrx, total, fin,
    swap_send, swap_recv, local_sem, plan_sem, in_sem,
    zg_send, zg_recv, zw_send, zw_recv, p1_send, p1_recv, p2_send, p2_recv, rx_send, rx_recv, zr_send, zr_recv,
):
    pair = lax.axis_index("pair")
    virt = lax.axis_index("virt")
    x, z = pair // NZ, pair % NZ
    y, c = virt // 2, virt % 2

    def at_z(d, other=0):
        return {"pair": x * NZ + (z + d + NZ) % NZ, "virt": y * 2 + (1 - c if other else c)}

    def at_x(d):
        return {"pair": (x + d) % NX * NZ + z, "virt": virt}

    def at_y(d):
        return {"pair": pair, "virt": (y + d) % NY * 2 + c}

    mate = {"pair": pair, "virt": y * 2 + 1 - c}

    def stage(s):
        return (stage_a, stage_b)[s // 8], s % 8

    def copy(src, dst, send, recv, device):
        return pltpu.make_async_remote_copy(
            src_ref=src, dst_ref=dst, send_sem=send, recv_sem=recv, device_id=device, device_id_type=MESH
        )

    sent = []

    def start(*what):
        one = copy(*what)
        one.start()
        sent.append(one)

    def arrived(ref, send, recv):
        copy(ref, ref, send, recv, mate).wait_recv()

    barrier = pltpu.get_barrier_semaphore()
    peers = [mate] + [at_z(d, other) for d in (2, -2, 1, -1) for other in (0, 1)]
    peers += [at_x(d) for d in (2, 1, 3)] + [at_y(d) for d in (2, 1, 3)]
    for peer in peers:
        pl.semaphore_signal(barrier, inc=1, device_id=peer, device_id_type=MESH)

    fetches = [
        pltpu.make_async_copy(source, target, in_sem.at[i])
        for i, (source, target) in enumerate(
            ((t2_hbm, t2_ref), (outs_hbm, outs_ref), (ins_hbm, ins_ref))
        )
    ]
    for one in fetches:
        one.start()
    local = pltpu.make_async_copy(tiles_ref, tiles.at[pl.ds(c * LIST, LIST)], local_sem)
    local.start()
    sums[SLOTS] = jnp.zeros((64, W), F32)
    for one in fetches:
        one.wait()

    for row in range(4):
        for j in range(8):
            at = (row % 2) * 8 + j
            rows[row // 2, at : at + 1, :] = t2_ref[row : row + 1, j * W : (j + 1) * W]
    stage_a[c, 0, 0, 0] = rows[c]
    lane = lax.broadcasted_iota(I32, (1, W), 1)
    pad = jnp.zeros((1, W - LIST), I32)
    key = jnp.concatenate([outs_ref[0] - y * 16, pad], axis=1) - c * 8
    key = jnp.where(lane < count_ref[0:1, 0:1], key, 8) + c * 9
    meta[c, 0:1, :] = key
    meta[c, 1:2, :] = jnp.concatenate([ins_ref[0], pad], axis=1)
    pl.semaphore_wait(barrier, len(peers))

    start(rows.at[1 - c], stage_a.at[c, 0, 0, 0], zg_send.at[0, 1], zg_recv.at[0, 1], mate)
    for d in (1, -1, 2, -2):
        at = SLOT_OF[-d]
        for other in (0, 1):
            part = rows.at[1 - c if other else c]
            start(part, stage_a.at[c, 0, 0, at], zg_send.at[at, other], zg_recv.at[at, other], at_z(d, other))
    start(meta.at[c], meta.at[c], swap_send.at[1], swap_recv.at[1], mate)

    def z_near(slot):
        if slot > 0:
            arrived(stage_a.at[c, 0, 0, slot], zg_send.at[slot, 0], zg_recv.at[slot, 0])
        arrived(stage_a.at[1 - c, 0, 0, slot], zg_send.at[slot, 1], zg_recv.at[slot, 1])

    def z_chunk(slot):
        ref, at = stage(slot)
        return ref.at[:, 0, 0, at]

    def z_pass(slot, d):
        at = SLOT_OF[DELTAS[slot] - d]
        start(z_chunk(slot), z_chunk(at), zg_send.at[at, 0], zg_recv.at[at, 0], at_z(d))

    def z_far(k):
        for slot in (SLOT_OF[-k], SLOT_OF[k])[: 1 if k == 8 else 2]:
            arrived(z_chunk(slot), zg_send.at[slot, 0], zg_recv.at[slot, 0])

    def whole(slot, piece):
        return stage_a.at[:, 0, pl.ds(1, 3), slot] if piece == 2 else stage_a.at[piece, pl.ds(1, 3), :, slot]

    def whole_start():
        for piece in range(3):
            for d in (1, -1):
                at = SLOT_OF[-d]
                start(whole(0, piece), whole(at, piece), zw_send.at[at - 1, piece], zw_recv.at[at - 1, piece], at_z(d))

    def whole_arrived():
        for piece in range(3):
            for at in (1, 2):
                arrived(whole(at, piece), zw_send.at[at - 1, piece], zw_recv.at[at - 1, piece])

    def first_at(h, g, at):
        ref, a = stage(GROUPS[g][0])
        slots = pl.ds(a, GROUPS[g][1] - GROUPS[g][0])
        return ref.at[0, 0, at, slots] if h == 0 else ref.at[1, at, 0, slots]

    def first_start(g):
        for d in (2, 1, 3):
            for h in range(2):
                sems = p1_send.at[h, g, d - 1], p1_recv.at[h, g, d - 1]
                start(first_at(h, g, 0), first_at(h, g, 4 - d), *sems, (at_x, at_y)[h](d))

    def first_arrived(g):
        for d in (1, 3, 2):
            for h in range(2):
                arrived(first_at(h, g, 4 - d), p1_send.at[h, g, d - 1], p1_recv.at[h, g, d - 1])

    def second_at(h, g, at, part):
        ref, a = stage(GROUPS[g][0])
        slots = pl.ds(a, GROUPS[g][1] - GROUPS[g][0])
        if h == 0:
            return ref.at[0, at, pl.ds(2 * part, 2), slots]
        return ref.at[1, pl.ds(2 * part, 2), at, slots]

    MOVES = ((0, 0, 1), (0, 1, 3), (0, 1, 1), (0, 0, 3), (3, 0, 1), (1, 1, 3))

    def second_start(g, k):
        at, part, d = MOVES[k]
        for h in range(2):
            sems = p2_send.at[h, g, k], p2_recv.at[h, g, k]
            start(second_at(h, g, at, part), second_at(h, g, (at + 4 - d) % 4, part), *sems, (at_y, at_x)[h](d))

    def second_arrived(g, k):
        at, part, d = MOVES[k]
        for h in range(2):
            arrived(second_at(h, g, (at + 4 - d) % 4, part), p2_send.at[h, g, k], p2_recv.at[h, g, k])

    def second_open(g):
        first_arrived(g)
        for k in range(4):
            second_start(g, k)

    def second_pass(g):
        for k in (0, 1):
            second_arrived(g, k)
            second_start(g, 4 + k)

    def halve(s, _):
        b = tiles[s]
        high = b.astype(BF)
        halves[s, :, :W] = high
        halves[s, :, W:] = (b - high.astype(F32)).astype(BF)
        return 0

    def halve_some(i):
        lax.fori_loop(i * 16, i * 16 + 16, halve, 0, unroll=2)

    flats = [ref.reshape(2 * 4 * 4 * 8 * 16, W) for ref in (stage_a, stage_b)]
    acc_rows = acc.reshape(2 * 16 * 64, W)
    rx_rows = rx.reshape(2 * 2 * 3 * 8 * 16, W)

    def products(g, h):
        def slot(k, running):
            n = plan[1, k]
            dy = (n // 16 + 4 - y) % 4
            a = flats[g][pl.ds((n // 8 % 2 * 4 + dy) * 512 + n % 8, 64, stride=8), :]
            keep = plan[2, k].astype(F32)
            high = a.astype(BF)
            a = jnp.concatenate([high, (a - high.astype(F32)).astype(BF)], axis=1)
            b = halves[plan[0, k]]
            product = jnp.dot(a, jnp.concatenate([b, b], axis=0), preferred_element_type=F32)
            running = running * keep + (product[:, :W] + product[:, W:])
            sums[k] = running
            return running

        lax.fori_loop(h * LIST, h * LIST + LIST, slot, jnp.zeros((64, W), F32), unroll=4)

        def pick(t, _):
            acc[g, t] = sums[plan[3, t]]
            return 0

        lax.fori_loop(h * 8, h * 8 + 8, pick, 0)
        for d in (2, 1, 3):
            part = acc.at[g, pl.ds(h * 8, 8), pl.ds(d * 16, 16), :]
            start(part, rx.at[g, h, 3 - d], rx_send.at[g, h, 3 - d], rx_recv.at[g, h, 3 - d], at_x(d))

    def add_up(g, h):
        for i in range(3):
            arrived(rx.at[g, h, i], rx_send.at[g, h, i], rx_recv.at[g, h, i])

        def add(s, _):
            for r in range(2):
                at = s * 2 + r
                value = acc_rows[pl.ds((g * 16 + h * 8) * 64 + at, 8, stride=64), :]
                for i in range(3):
                    value += rx_rows[pl.ds(((g * 2 + h) * 3 + i) * 128 + at, 8, stride=16), :]
                zbuf[h, g * 8 + s, r * 8 : r * 8 + 8, :] = value
            return 0

        lax.fori_loop(0, 8, add, 0, unroll=2)
        for s in range(g * 8 + 7, max(g * 8 - 1, 0), -1):
            back = SLOT_OF[-DELTAS[s]]
            start(zbuf.at[h, s], zrx.at[h, back], zr_send.at[h, back], zr_recv.at[h, back], at_z(DELTAS[s]))

    z_near(0)
    first_start(0)
    start(tiles_ref, tiles.at[pl.ds(c * LIST, LIST)], swap_send.at[2], swap_recv.at[2], mate)
    for k in (1, -1):
        z_near(SLOT_OF[k])
        z_pass(SLOT_OF[k], -2 * k)
    for k in (2, -2):
        z_near(SLOT_OF[k])
        z_pass(SLOT_OF[k], -k)
    first_start(1)
    for k in (1, -1, 2, -2):
        z_pass(SLOT_OF[k], -4 if k > 0 else 4)
    second_open(0)

    arrived(meta.at[1 - c], swap_send.at[1], swap_recv.at[1])
    low = lane < LIST
    both = [jnp.where(low, meta[0, k : k + 1, :], pltpu.roll(meta[1, k : k + 1, :], LIST, 1)) for k in range(2)]
    schedule(jnp.where(lane < SLOTS, both[0], 18), both[1], sched)
    turn = pltpu.make_async_copy(sched, plan, plan_sem)
    turn.start()

    z_far(3)
    z_pass(SLOT_OF[3], -4)
    z_pass(SLOT_OF[-3], 4)
    z_far(4)
    z_pass(SLOT_OF[-4], 4)
    first_start(2)
    second_pass(0)
    second_open(1)
    for k in range(2, 6):
        second_arrived(0, k)
    whole_start()
    z_far(5)
    z_far(6)
    first_start(3)
    local.wait()
    arrived(tiles.at[pl.ds((1 - c) * LIST, LIST)], swap_send.at[2], swap_recv.at[2])
    halve_some(0)
    second_pass(1)
    second_open(2)
    halve_some(1)
    z_far(7)
    z_far(8)
    first_start(4)
    halve_some(2)
    second_open(3)
    halve_some(3)
    turn.wait()
    second_pass(2)
    second_open(4)
    whole_arrived()
    for g in (1, 2):
        for k in range(2, 6):
            second_arrived(g, k)
    products(0, 0)
    second_pass(3)
    products(0, 1)
    second_pass(4)
    add_up(0, 0)
    add_up(0, 1)
    for g in (3, 4):
        for k in range(2, 6):
            second_arrived(g, k)
    for h in range(2):
        products(1, h)
    for h in range(2):
        add_up(1, h)

    for h in range(2):
        value = zbuf[h, 0]
        for s in range(1, NZ):
            arrived(zrx.at[h, s], zr_send.at[h, s], zr_recv.at[h, s])
            value += zrx[h, s]
        total[h] = value

    fin[c] = total[c]
    start(total.at[1 - c], fin.at[c], swap_send.at[3], swap_recv.at[3], mate)
    arrived(fin.at[1 - c], swap_send.at[3], swap_recv.at[3])
    for row in range(4):
        for j in range(8):
            at = (row % 2) * 8 + j
            out_ref[row : row + 1, j * W : (j + 1) * W] = fin[row // 2, at : at + 1, :]

    for one in sent:
        one.wait_send()


def shards(t2_amplitudes, integral_tiles, out_tiles, in_tiles, tile_counts):
    vmem = pl.BlockSpec(memory_space=pltpu.VMEM)
    dma = pltpu.SemaphoreType.DMA
    return pl.pallas_call(
        kernel,
        out_shape=jax.ShapeDtypeStruct(t2_amplitudes.shape, F32),
        in_specs=[pl.BlockSpec(memory_space=pltpu.HBM)] * 4 + [vmem],
        out_specs=vmem,
        scratch_shapes=[
            pltpu.VMEM(t2_amplitudes.shape, F32),
            pltpu.VMEM(out_tiles.shape, I32),
            pltpu.VMEM(in_tiles.shape, I32),
            pltpu.VMEM((2, 16, W), F32),
            pltpu.VMEM((2, NY, NX, 8, 16, W), F32),
            pltpu.VMEM((2, NY, NX, 8, 16, W), F32),
            pltpu.VMEM((SLOTS, W, W), F32),
            pltpu.VMEM((SLOTS, W, 2 * W), BF),
            pltpu.VMEM((2, 8, W), I32),
            pltpu.VMEM((8, W), I32),
            pltpu.SMEM((8, W), I32),
            pltpu.VMEM((SLOTS + 1, 64, W), F32),
            pltpu.VMEM((2, 16, 64, W), F32),
            pltpu.VMEM((2, 2, 3, 8, 16, W), F32),
            pltpu.VMEM((2, NZ, 16, W), F32),
            pltpu.VMEM((2, NZ, 16, W), F32),
            pltpu.VMEM((2, 16, W), F32),
            pltpu.VMEM((2, 16, W), F32),
            dma((4,)), dma((4,)), dma, dma, dma((3,)),
            dma((NZ, 2)), dma((NZ, 2)), dma((2, 3)), dma((2, 3)), dma((2, NG, 3)), dma((2, NG, 3)), dma((2, NG, 6)), dma((2, NG, 6)),
            dma((2, 2, 3)), dma((2, 2, 3)), dma((2, NZ)), dma((2, NZ)),
        ],
        compiler_params=pltpu.CompilerParams(
            collective_id=0, has_side_effects=True, vmem_limit_bytes=62 * 1024 * 1024
        ),
    )(t2_amplitudes, integral_tiles.reshape(LIST, W, W), out_tiles, in_tiles, tile_counts)


def solution(mesh):
    return jax.shard_map(
        shards,
        mesh=mesh,
        in_specs=(
            P("pair", "virt"),
            P("pair", "virt", None, None, None),
            P("pair", "virt", None),
            P("pair", "virt", None),
            P("pair", "virt"),
        ),
        out_specs=P("pair", "virt"),
        check_vma=False,
    )
```

time: 80.1 us -> 74.5 us (0.930)
  Pallas kernels: 77.9 us -> 72.2 us
    pallas_call x1, Pallas kernels: 77.9 us -> 72.2 us  [shards(): pl.pallas_call(kernel, out_shape=jax.ShapeDtypeStruct(t2_amplitudes.shape...]
where the time goes in v3:
time: 74.5 us; the launch traced here: 74.2 us
  Pallas kernels  72.2 us (97%)
  local copies, waits for them, and re-layouts  1.32 us (2%)
    pallas_call x1, Pallas kernels, shards(): pl.pallas_call(kernel, out_shape=jax.ShapeDtypeStruct(t2_amplitudes.shape...  72.2 us

profile of v3, /device:TPU:1, one launch (start us, length us, event | category | flops | bytes accessed | tf_op | source)
XLA Modules:
  0.0 74.2 jit_solution(4516449467327961779)
XLA Ops:
  0.7 72.2 %shard_map.55 = f32[4,1024]{1,0:T(4,128)} custom-call(f32[4,1024]{1,0:T(4,128)} %t2_hbm.1, f32[32,128,128]{2,1,0:T(8,128)} %bitcast.1, s32[1,1,32]{2,1,0:T(1,128)} %outs_hbm.1, s32[1,1,32]{2,1,0:T(1,128)} %ins_hbm.1, s32[1,1]{1,0:T(1,128)S(6)} %copy.7.count_ref), custom_call_target="tpu_custom_call" | custom-call | tf_op jit(solution)/shard_map/pallas_call | solution.py:349
  72.8 1.3 %copy.8 = f32[4,1024]{1,0:T(4,128)} copy(f32[4,1024]{1,0:T(4,128)} %shard_map.55) | data formatting | bytes 32768

commit v4 on v3

--- a/solution.py
+++ b/solution.py
@@ -15,10 +15,10 @@
 F32 = jnp.float32
 I32 = jnp.int32
 BF = jnp.bfloat16
-DELTAS = (0, 1, -1, 2, -2, 3, -3, 4, -4, 5, -5, 6, -6, 7, -7, 8)
+DELTAS = (0, 1, -1, 2, -2, 7, -7, 8, 3, -3, 4, -4, 5, -5, 6, -6)
 SLOT_OF = {d: i for i, d in enumerate(DELTAS)}
 SLOT_OF[-8] = SLOT_OF[8]
-GROUPS = ((0, 1), (3, 5), (5, 8), (8, 13), (13, 16))
+GROUPS = ((0, 1), (3, 5), (5, 8), (8, 12), (12, 16))
 NG = len(GROUPS)
 
 
@@ -119,13 +119,15 @@
         at = SLOT_OF[-d]
         for other in (0, 1):
             part = rows.at[1 - c if other else c]
-            start(part, stage_a.at[c, 0, 0, at], zg_send.at[at, other], zg_recv.at[at, other], at_z(d, other))
+            ref, slot = stage(at)
+            start(part, ref.at[c, 0, 0, slot], zg_send.at[at, other], zg_recv.at[at, other], at_z(d, other))
     start(meta.at[c], meta.at[c], swap_send.at[1], swap_recv.at[1], mate)
 
     def z_near(slot):
+        ref, at = stage(slot)
         if slot > 0:
-            arrived(stage_a.at[c, 0, 0, slot], zg_send.at[slot, 0], zg_recv.at[slot, 0])
-        arrived(stage_a.at[1 - c, 0, 0, slot], zg_send.at[slot, 1], zg_recv.at[slot, 1])
+            arrived(ref.at[c, 0, 0, at], zg_send.at[slot, 0], zg_recv.at[slot, 0])
+        arrived(ref.at[1 - c, 0, 0, at], zg_send.at[slot, 1], zg_recv.at[slot, 1])
 
     def z_chunk(slot):
         ref, at = stage(slot)
@@ -227,7 +229,7 @@
             sums[k] = running
             return running
 
-        lax.fori_loop(h * LIST, h * LIST + LIST, slot, jnp.zeros((64, W), F32), unroll=4)
+        lax.fori_loop(h * LIST, h * LIST + LIST, slot, jnp.zeros((64, W), F32), unroll=8)
 
         def pick(t, _):
             acc[g, t] = sums[plan[3, t]]
@@ -252,7 +254,7 @@
             return 0
 
         lax.fori_loop(0, 8, add, 0, unroll=2)
-        for s in range(g * 8 + 7, max(g * 8 - 1, 0), -1):
+        for s in sorted(range(max(g * 8, 1), g * 8 + 8), key=lambda s: -abs(DELTAS[s])):
             back = SLOT_OF[-DELTAS[s]]
             start(zbuf.at[h, s], zrx.at[h, back], zr_send.at[h, back], zr_recv.at[h, back], at_z(DELTAS[s]))
 
@@ -282,7 +284,7 @@
     z_pass(SLOT_OF[-3], 4)
     z_far(4)
     z_pass(SLOT_OF[-4], 4)
-    first_start(2)
+    first_start(3)
     second_pass(0)
     second_open(1)
     for k in range(2, 6):
@@ -290,39 +292,39 @@
     whole_start()
     z_far(5)
     z_far(6)
-    first_start(3)
+    first_start(4)
     local.wait()
     arrived(tiles.at[pl.ds((1 - c) * LIST, LIST)], swap_send.at[2], swap_recv.at[2])
     halve_some(0)
     second_pass(1)
-    second_open(2)
+    second_open(3)
     halve_some(1)
     z_far(7)
     z_far(8)
-    first_start(4)
+    first_start(2)
     halve_some(2)
-    second_open(3)
+    second_open(4)
     halve_some(3)
+    second_pass(3)
+    second_open(2)
     turn.wait()
+    second_pass(4)
+    for g in (3, 4):
+        for k in range(2, 6):
+            second_arrived(g, k)
     second_pass(2)
-    second_open(4)
+    products(1, 0)
+    products(1, 1)
     whole_arrived()
     for g in (1, 2):
         for k in range(2, 6):
             second_arrived(g, k)
     products(0, 0)
-    second_pass(3)
+    add_up(1, 0)
     products(0, 1)
-    second_pass(4)
-    add_up(0, 0)
-    add_up(0, 1)
-    for g in (3, 4):
-        for k in range(2, 6):
-            second_arrived(g, k)
+    add_up(1, 1)
     for h in range(2):
-        products(1, h)
-    for h in range(2):
-        add_up(1, h)
+        add_up(0, h)
 
     for h in range(2):
         value = zbuf[h, 0]

time: 74.5 us -> 73.3 us (0.984)
  Pallas kernels: 72.2 us -> 71 us
    pallas_call x1, Pallas kernels: 72.2 us -> 71 us  [shards(): pl.pallas_call(kernel, out_shape=jax.ShapeDtypeStruct(t2_amplitudes.shape...]
where the time goes in v4:
time: 73.3 us; the launch traced here: 73 us
  Pallas kernels  71 us (97%)
  local copies, waits for them, and re-layouts  1.32 us (2%)
    pallas_call x1, Pallas kernels, shards(): pl.pallas_call(kernel, out_shape=jax.ShapeDtypeStruct(t2_amplitudes.shape...  71 us

profile of v4, /device:TPU:1, one launch (start us, length us, event | category | flops | bytes accessed | tf_op | source)
XLA Modules:
  0.0 73.0 jit_solution(632912281484488281)
XLA Ops:
  0.7 71.0 %shard_map.55 = f32[4,1024]{1,0:T(4,128)} custom-call(f32[4,1024]{1,0:T(4,128)} %t2_hbm.1, f32[32,128,128]{2,1,0:T(8,128)} %bitcast.1, s32[1,1,32]{2,1,0:T(1,128)} %outs_hbm.1, s32[1,1,32]{2,1,0:T(1,128)} %ins_hbm.1, s32[1,1]{1,0:T(1,128)S(6)} %copy.7.count_ref), custom_call_target="tpu_custom_call" | custom-call | tf_op jit(solution)/shard_map/pallas_call | solution.py:351
  71.7 1.3 %copy.8 = f32[4,1024]{1,0:T(4,128)} copy(f32[4,1024]{1,0:T(4,128)} %shard_map.55) | data formatting | bytes 32768

commit v5 on v4

--- a/solution.py
+++ b/solution.py
@@ -43,7 +43,7 @@
 
 def kernel(
     t2_hbm, tiles_ref, outs_hbm, ins_hbm, count_ref, out_ref,
-    t2_ref, outs_ref, ins_ref, rows, stage_a, stage_b, tiles, halves, meta, sched, plan, sums, acc, rx, zbuf, zrx, total, fin,
+    t2_ref, outs_ref, ins_ref, rows, stage_a, stage_b, tiles, halves, meta, sched, plan, sums, acc, rx, zbuf, zrx, fin,
     swap_send, swap_recv, local_sem, plan_sem, in_sem,
     zg_send, zg_recv, zw_send, zw_recv, p1_send, p1_recv, p2_send, p2_recv, rx_send, rx_recv, zr_send, zr_recv,
 ):
@@ -256,7 +256,8 @@
         lax.fori_loop(0, 8, add, 0, unroll=2)
         for s in sorted(range(max(g * 8, 1), g * 8 + 8), key=lambda s: -abs(DELTAS[s])):
             back = SLOT_OF[-DELTAS[s]]
-            start(zbuf.at[h, s], zrx.at[h, back], zr_send.at[h, back], zr_recv.at[h, back], at_z(DELTAS[s]))
+            owner = {"pair": at_z(DELTAS[s])["pair"], "virt": y * 2 + h}
+            start(zbuf.at[h, s], zrx.at[c, back], zr_send.at[h, back], zr_recv.at[c, back], owner)
 
     z_near(0)
     first_start(0)
@@ -326,16 +327,16 @@
     for h in range(2):
         add_up(0, h)
 
-    for h in range(2):
-        value = zbuf[h, 0]
+    zrx[c, 0] = zbuf[c, 0]
+    start(zbuf.at[1 - c, 0], zrx.at[c, 0], swap_send.at[3], swap_recv.at[3], mate)
+    arrived(zrx.at[1 - c, 0], swap_send.at[3], swap_recv.at[3])
+    for half in range(2):
+        value = zrx[half, 0]
         for s in range(1, NZ):
-            arrived(zrx.at[h, s], zr_send.at[h, s], zr_recv.at[h, s])
-            value += zrx[h, s]
-        total[h] = value
-
-    fin[c] = total[c]
-    start(total.at[1 - c], fin.at[c], swap_send.at[3], swap_recv.at[3], mate)
-    arrived(fin.at[1 - c], swap_send.at[3], swap_recv.at[3])
+            arrived(zrx.at[half, s], zr_send.at[half, s], zr_recv.at[half, s])
+            value += zrx[half, s]
+        fin[half] = value
+
     for row in range(4):
         for j in range(8):
             at = (row % 2) * 8 + j
@@ -371,7 +372,6 @@
             pltpu.VMEM((2, NZ, 16, W), F32),
             pltpu.VMEM((2, NZ, 16, W), F32),
             pltpu.VMEM((2, 16, W), F32),
-            pltpu.VMEM((2, 16, W), F32),
             dma((4,)), dma((4,)), dma, dma, dma((3,)),
             dma((NZ, 2)), dma((NZ, 2)), dma((2, 3)), dma((2, 3)), dma((2, NG, 3)), dma((2, NG, 3)), dma((2, NG, 6)), dma((2, NG, 6)),
             dma((2, 2, 3)), dma((2, 2, 3)), dma((2, NZ)), dma((2, NZ)),

time: 73.3 us -> 72 us (0.982)
  Pallas kernels: 71 us -> 69.8 us
    pallas_call x1, Pallas kernels: 71 us -> 69.8 us  [shards(): pl.pallas_call(kernel, out_shape=jax.ShapeDtypeStruct(t2_amplitudes.shape...]
where the time goes in v5:
time: 72 us; the launch traced here: 71.7 us
  Pallas kernels  69.8 us (97%)
  local copies, waits for them, and re-layouts  1.32 us (2%)
    pallas_call x1, Pallas kernels, shards(): pl.pallas_call(kernel, out_shape=jax.ShapeDtypeStruct(t2_amplitudes.shape...  69.8 us

profile of v5, /device:TPU:1, one launch (start us, length us, event | category | flops | bytes accessed | tf_op | source)
XLA Modules:
  0.0 71.7 jit_solution(17265516322698741935)
XLA Ops:
  0.7 69.8 %shard_map.55 = f32[4,1024]{1,0:T(4,128)} custom-call(f32[4,1024]{1,0:T(4,128)} %t2_hbm.1, f32[32,128,128]{2,1,0:T(8,128)} %bitcast.1, s32[1,1,32]{2,1,0:T(1,128)} %outs_hbm.1, s32[1,1,32]{2,1,0:T(1,128)} %ins_hbm.1, s32[1,1]{1,0:T(1,128)S(6)} %copy.7.count_ref), custom_call_target="tpu_custom_call" | custom-call | tf_op jit(solution)/shard_map/pallas_call | solution.py:352
  70.4 1.3 %copy.8 = f32[4,1024]{1,0:T(4,128)} copy(f32[4,1024]{1,0:T(4,128)} %shard_map.55) | data formatting | bytes 32768
